TPU v7x, 512 devices: a whole 4x8x8 slice. The times are simulated.
512 devices in a mesh: dp: 64 (over y, x, core), mp: 8 (over z).
Axes of the slice: x: 4, y: 8, z: 8, core: 2. Of those that a mesh axis runs over, the one named last changes fastest.
Arguments:
- tokens: bfloat16 [32768, 2048], P('dp'), may hold values from -6 to 6
- q_weight: bfloat16 [2048, 256], P('dp', 'mp'), may hold values from -0.125 to 0.125
- k_weight: bfloat16 [2048, 256], P('dp', 'mp'), may hold values from -0.125 to 0.125
- v_weight: bfloat16 [2048, 2048], P('dp', 'mp'), may hold values from -0.125 to 0.125
- adapter_down: bfloat16 [2048, 256], P(None, 'mp'), may hold values from -0.125 to 0.125
- adapter_up: bfloat16 [256, 2048], P(None, 'mp'), may hold values from -1.5 to 1.5
- lengths: int32 [4], replicated, may hold values from 1 to 16384, 32768 in all
- adapter_ids: int32 [4], replicated, may hold values from 0 to 15
- head_gain: float32 [2048], P('mp'), may hold values from 0.1 to 1.9
- out_weight: bfloat16 [2048, 2048], P('mp', 'dp'), may hold values from -0.125 to 0.125
Outputs:
- layer_out: bfloat16 [32768, 2048], P('dp', 'mp')
Inputs may be any that keep to these rules, and one draw needn't show every extreme that they name: The lengths sum to 32768 and the longest request has exactly 32768 // 2 tokens.
All inputs are finite; a program needn't handle non-finite values.
Results may differ from a plain program's by a relative error of at most 0.022.
Values may be sent and summed in bfloat16 or wider, within the bound.
A program may use at most 128 MiB of HBM per device.

v0:
```python
import math
import jax
import jax.numpy as jnp
from jax import lax
from jax.sharding import PartitionSpec as P

F = 16
R = 16
EPSILON = 1e-05


def taylor(inputs):
    squares = (inputs[..., :, None] * inputs[..., None, :]).reshape(
        inputs.shape[:-1] + (inputs.shape[-1] * inputs.shape[-1],)
    )
    constant = jnp.ones(inputs.shape[:-1] + (1,), jnp.float32)
    return jnp.concatenate([constant, 0.5 * inputs, squares * (0.25 / math.sqrt(2.0))], axis=-1)


def request_of(bounds, positions):
    return jnp.sum((positions[:, None] >= bounds[None, :]).astype(jnp.int32), axis=1)


def token_tables(lengths, adapter_ids, positions):
    bounds = jnp.cumsum(lengths)
    request = request_of(bounds, positions)
    openings = bounds - lengths
    starts = jnp.any(positions[:, None] == openings[None, :], axis=1)
    picked = request[:, None] == jnp.arange(lengths.shape[0], dtype=jnp.int32)[None, :]
    adapter = jnp.sum(jnp.where(picked, adapter_ids[None, :], 0), axis=1)
    return (request, starts, adapter)


def block_local(query, key_rows, values, request, starts):
    scores = jnp.einsum("ihd,jhd->hij", query, key_rows, preferred_element_type=jnp.float32) * 0.25
    weights = 1.0 + scores + 0.5 * scores * scores
    indexes = jnp.arange(request.shape[0], dtype=jnp.int32)
    allowed = (indexes[None, :] <= indexes[:, None]) & (request[None, :] == request[:, None])
    weights = jnp.where(allowed[None], weights, 0.0).astype(jnp.bfloat16)
    within = jnp.einsum("hij,jhe->ihe", weights, values, preferred_element_type=jnp.float32)
    query_map = taylor(query.astype(jnp.float32)).astype(jnp.bfloat16)
    key_map = taylor(key_rows.astype(jnp.float32)).astype(jnp.bfloat16)
    tail_mask = (request == request[-1]).astype(jnp.bfloat16)
    masked_keys = key_map * tail_mask[:, None, None]
    summary = jnp.einsum("ihf,ihe->hfe", masked_keys, values, preferred_element_type=jnp.float32)
    return (within, query_map, summary)


def finish(within, query_map, carried, request, starts, gains):
    follows = ((request == request[0]) & jnp.logical_not(starts[0])).astype(jnp.float32)
    cross = jnp.einsum(
        "ihf,hfe->ihe", query_map, carried.astype(jnp.bfloat16), preferred_element_type=jnp.float32
    )
    combined = within + follows[:, None, None] * cross
    factor = lax.rsqrt(jnp.mean(combined * combined, axis=-1, keepdims=True) + EPSILON)
    return (combined * factor * gains[None]).astype(jnp.bfloat16)


def carry_weights(lengths, row_count, place, blocks):
    bounds = jnp.cumsum(lengths)
    firsts = jnp.arange(blocks, dtype=jnp.int32) * row_count
    tails = request_of(bounds, firsts + (row_count - 1))
    head = request_of(bounds, place[None] * row_count)[0]
    chosen = (jnp.arange(blocks, dtype=jnp.int32) < place) & (tails == head)
    return chosen.astype(jnp.bfloat16)


def per_device(
    tokens,
    q_weight,
    k_weight,
    v_weight,
    adapter_down,
    adapter_up,
    lengths,
    adapter_ids,
    head_gain,
    out_weight,
):
    row_count = tokens.shape[0]
    qf = q_weight.shape[1]
    heads_here = qf // F
    vw = v_weight.shape[1]
    value_width = vw // heads_here
    blocks = lax.axis_size("dp")
    place = lax.axis_index("dp")
    positions = place * row_count + jnp.arange(row_count, dtype=jnp.int32)
    request, starts, adapter = token_tables(lengths, adapter_ids, positions)
    local = jnp.concatenate([q_weight, k_weight, v_weight, out_weight.T], axis=1)
    gathered = lax.all_gather(local, "dp", axis=0, tiled=True)
    q_full = gathered[:, :qf]
    k_full = gathered[:, qf : 2 * qf]
    v_full = gathered[:, 2 * qf : 2 * qf + vw]
    out_t = gathered[:, 2 * qf + vw :]
    part_low = jnp.dot(tokens, adapter_down, preferred_element_type=jnp.float32)
    owners = (
        lax.axis_index("mp") * (adapter_down.shape[1] // R)
        + jnp.arange(adapter_down.shape[1], dtype=jnp.int32) // R
    )
    part_low = jnp.where(adapter[:, None] == owners[None, :], part_low, 0.0).astype(jnp.bfloat16)
    low_rank = lax.all_gather(part_low, "mp", axis=1, tiled=True)
    query_sum = jnp.dot(tokens, q_full, preferred_element_type=jnp.float32)
    key_sum = jnp.dot(tokens, k_full, preferred_element_type=jnp.float32)
    value_sum = jnp.dot(tokens, v_full, preferred_element_type=jnp.float32)
    query = query_sum.astype(jnp.bfloat16).reshape(row_count, heads_here, F)
    key_rows = key_sum.astype(jnp.bfloat16).reshape(row_count, heads_here, F)
    values = value_sum + jnp.dot(low_rank, adapter_up, preferred_element_type=jnp.float32)
    values = values.astype(jnp.bfloat16).reshape(row_count, heads_here, value_width)
    within, query_map, summary = block_local(query, key_rows, values, request, starts)
    every = lax.all_gather(summary.astype(jnp.bfloat16), "dp")
    chosen = carry_weights(lengths, row_count, place, blocks)
    carried = jnp.dot(
        chosen[None, :], every.reshape(blocks, -1), preferred_element_type=jnp.float32
    ).reshape(summary.shape)
    gains = head_gain.reshape(heads_here, value_width)
    normed = finish(within, query_map, carried, request, starts, gains).reshape(
        row_count, heads_here * value_width
    )
    partial_terms = lax.dot_general(
        normed, out_t, (((1,), (1,)), ((), ())), preferred_element_type=jnp.float32
    )
    return lax.psum_scatter(
        partial_terms.astype(jnp.bfloat16), "mp", scatter_dimension=1, tiled=True
    )


def solution(mesh):
    placed = (
        P("dp", None),
        P("dp", "mp"),
        P("dp", "mp"),
        P("dp", "mp"),
        P(None, "mp"),
        P(None, "mp"),
        P(),
        P(),
        P("mp"),
        P("mp", "dp"),
    )
    return jax.shard_map(
        per_device, mesh=mesh, in_specs=placed, out_specs=P("dp", "mp"), check_vma=False
    )
```

profile of v0, /device:TPU:2, one launch (start us, length us, event | category | flops | bytes accessed | tf_op | source)
XLA Modules:
  0.0 274.3 jit_solution(4233398418461733872)
XLA Ops:
  6.5 0.0 copy-start
  6.5 0.0 copy-start.1
  6.5 0.0 all-gather.4.cloned.1.call-start
  6.5 1.6 pad_maximum_fusion
  8.1 0.0 all-gather.4.cloned.1.call-update
  8.2 0.0 all-gather.6.cloned.1.call-start
  8.2 0.8 reduce-window.4
  9.1 0.7 bitcast_subtract_fusion
  9.7 0.1 compare_reduce_fusion
  9.9 0.1 convert_reduce_fusion
  10.0 0.7 fusion.43
  10.6 0.7 select_reduce_fusion
  11.4 0.0 copy-done
  11.4 1.6 fusion.7
  13.0 31.1 %all_gather.13 = bf16[512,256]{0,1:T(8,128)(2,1)S(1)} all-gather(bf16[512,32]{0,1:T(8,128)(2,1)S(1)} %fusion.7), channel_id=1, replica_groups=mesh['dp'=64,'mp'=8] {'mp'}, dimensions={1}, use_global_device_ids=true | all-gather | bytes 294912 | tf_op jit(solution)/shard_map/all_gather | solution.py:101
  44.2 1.3 compare_convert_fusion
  45.4 0.0 copy-done.1
  45.4 0.3 fusion.44
  45.7 51.4 %all-gather.4.cloned.1.call-done = bf16[2048,576]{1,0:T(8,128)(2,1)} async-done(((bf16[32,576]{1,0:T(8,128)(2,1)}), bf16[2048,576]{1,0:T(8,128)(2,1)}) %all-gather.4.cloned.1.call-update) | async-done | bytes 2359312 | tf_op jit(solution)/shard_map/all_gather | solution.py:90
  97.1 2.1 convolution_convert_fusion.2
  99.3 0.1 multiply_convert_fusion.1
  99.4 2.5 fusion.6
  101.9 1.1 convolution_convert_fusion.1
  103.0 0.0 all-gather.6.cloned.1.call-update
  103.1 0.0 reduce-scatter.2.cloned.1.call-start
  103.1 0.6 fusion.33
  103.8 0.1 convert_reduce_fusion.1
  103.9 0.2 fusion.14
  104.1 1.8 convolution_convert_fusion.3
  105.9 0.1 multiply_convert_fusion
  106.0 1.8 fusion.2
  107.8 82.7 %all-gather.6.cloned.1.call-done = bf16[128,273,128]{2,1,0:T(8,128)(2,1)} async-done(((bf16[2,273,128]{2,1,0:T(8,128)(2,1)}), bf16[128,273,128]{2,1,0:T(8,128)(2,1)}) %all-gather.6.cloned.1.call-update) | async-done | bytes 8945680 | tf_op jit(solution)/shard_map/all_gather | solution.py:110
  190.5 10.9 %reshape.177 = bf16[64,69888]{1,0:T(8,128)(2,1)} reshape(bf16[128,273,128]{2,1,0:T(8,128)(2,1)} %all-gather.6.cloned.1.call-done) | data formatting | bytes 17891328 | tf_op jit(solution)/shard_map/reshape | solution.py:113
  201.4 11.1 %dot_general.49 = bf16[2,273,128,64]{2,1,0,3:T(8,128)(2,1)} reshape(bf16[69888,64]{0,1:T(8,128)(2,1)} %bitcast.53) | data formatting | bytes 17891328 | tf_op jit(solution)/shard_map/dot_general | solution.py:112
  212.5 0.0 copy-start.3
  212.5 5.8 %fusion = bf16[1,2,273,128]{3,0,2,1:T(2,128)(2,1)S(1)} fusion(bf16[2,273,128,64]{2,1,0,3:T(8,128)(2,1)} %dot_general.49, s32[64]{0:T(128)S(1)} %convert_reduce_fusion.1, s32[]{:T(128)} %fusion.33, s32[]{:T(128)S(6)} %axis_index.23), kind=kOutput, calls=%fused_computation | convolution fusion | flops 8945856 | bytes 9085704 | tf_op jit(solution)/shard_map/dot_general | solution.py:112
  218.3 0.0 copy-start.2
  218.3 0.0 copy-done.3
  218.3 0.5 multiply_reduce_fusion
  218.8 0.1 copy-done.2
  219.0 0.1 multiply_convert_fusion.2
  219.1 3.9 %convolution_convert_fusion = bf16[512,2048]{1,0:T(8,128)(2,1)} fusion(bf16[512,256]{0,1:T(8,128)(2,1)S(1)} %bitcast.54, bf16[2048,576]{1,0:T(8,128)(2,1)} %all-gather.4.cloned.1.call-done), kind=kOutput, calls=%fused_computation.2 | convolution fusion | flops 537919488 | bytes 3407872 | tf_op jit(solution)/shard_map/dot_general | solution.py:119
  223.0 0.0 reduce-scatter.2.cloned.1.call-update
  223.0 44.7 %reduce-scatter.2.cloned.1.call-done = bf16[512,256]{1,0:T(8,128)(2,1)} async-done(((bf16[512,2048]{1,0:T(8,128)(2,1)}), bf16[512,256]{1,0:T(8,128)(2,1)}) %reduce-scatter.2.cloned.1.call-update) | async-done | bytes 262160 | tf_op jit(solution)/shard_map/reduce_scatter | solution.py:122
  (9 shorter events, 0.1 us)
Async XLA Ops:
  6.5 4.8 %copy-start = (bf16[512,2048]{1,0:T(8,128)(2,1)S(1)}, bf16[512,2048]{1,0:T(8,128)(2,1)}, u32[]{:S(2)}) copy-start(bf16[512,2048]{1,0:T(8,128)(2,1)} %param.10) | copy-start | bytes 6291460
  6.5 38.9 %copy-start.1 = (bf16[256,256]{1,0:T(8,128)(2,1)S(1)}, bf16[256,256]{1,0:T(8,128)(2,1)}, u32[]{:S(2)}) copy-start(bf16[256,256]{1,0:T(8,128)(2,1)} %param.15) | copy-start | bytes 393220
  6.5 90.6 %all-gather.4.cloned.1.call-start = ((), (), s32[]{:S(2)}) async-start(), calls=%async_computation.1 | async-start | bytes 2662400 | tf_op jit(solution)/shard_map/all_gather | solution.py:90
  8.2 182.3 %all-gather.6.cloned.1.call-start = ((), (), s32[]{:S(2)}) async-start(), calls=%async_computation.3 | async-start | bytes 9318400 | tf_op jit(solution)/shard_map/all_gather | solution.py:110
  103.1 164.7 %reduce-scatter.2.cloned.1.call-start = ((), (), s32[]{:S(2)}) async-start(), calls=%async_computation.2 | async-start | bytes 2359296 | tf_op jit(solution)/shard_map/reduce_scatter | solution.py:122
  212.5 5.8 %copy-start.3 = (f32[2,128,512]{2,1,0:T(8,128)S(1)}, f32[2,128,512]{2,1,0:T(8,128)}, u32[]{:S(2)}) copy-start(f32[2,128,512]{2,1,0:T(8,128)} %fusion.2) | copy-start | bytes 1572868
  218.3 0.7 copy-start.2
Sparse Core Ops, SparseCore 0:
  10.7 86.4 all-gather.3
  103.2 87.2 all-gather.5
  223.1 44.5 reduce-scatter.1
where the time goes:
time: 275 us; the launch traced here: 274 us
  waiting for transfers between devices  179 us (65%)
  blocking collectives  31.1 us (11%)
  local copies, waits for them, and re-layouts  22.8 us (8%)
  matrix products  21.4 us (8%)
  between operations  13.3 us (5%)
  other arithmetic  6.59 us (2%)
    all_gather x1, waiting for transfers between devices, per_device(): every = lax.all_gather(summary.astype(jnp.bfloat16), 'dp')  82.7 us
    all_gather x1, waiting for transfers between devices, per_device(): gathered = lax.all_gather(local, 'dp', axis=0, tiled=True)  51.4 us
    reduce_scatter x1, waiting for transfers between devices, per_device(): lax.psum_scatter(partial_terms.astype(jnp.bfloat16), 'mp', scatter_dimens...  44.7 us
    all_gather x1, blocking collectives, per_device(): low_rank = lax.all_gather(part_low, 'mp', axis=1, tiled=True)  31.1 us
    dot_general x1, local copies, waits for them, and re-layouts, per_device(): jnp.dot(chosen[None, :], every.reshape(blocks, -1), preferred_element_typ...  11.1 us
    reshape x1, local copies, waits for them, and re-layouts, per_device(): every.reshape(blocks, -1)  10.9 us
    dot_general x1, matrix products, per_device(): jnp.dot(chosen[None, :], every.reshape(blocks, -1), preferred_element_typ...  5.76 us
  transfers between devices with their start and end apart: 3, of which 3 were waited for; matrix products, arithmetic and copies ran while one was open for 4% of the time, Pallas kernels for 0%

commit v1 on v0

--- a/solution.py
+++ b/solution.py
@@ -7,6 +7,11 @@
 F = 16
 R = 16
 EPSILON = 1e-05
+
+
+def tiled_gather(array, axis, dim):
+    copies = jnp.concatenate([array] * lax.axis_size(axis), axis=dim)
+    return lax.all_to_all(copies, axis, dim, dim, tiled=True)
 
 
 def taylor(inputs):
@@ -98,7 +103,7 @@
         + jnp.arange(adapter_down.shape[1], dtype=jnp.int32) // R
     )
     part_low = jnp.where(adapter[:, None] == owners[None, :], part_low, 0.0).astype(jnp.bfloat16)
-    low_rank = lax.all_gather(part_low, "mp", axis=1, tiled=True)
+    low_rank = tiled_gather(part_low, "mp", 1)
     query_sum = jnp.dot(tokens, q_full, preferred_element_type=jnp.float32)
     key_sum = jnp.dot(tokens, k_full, preferred_element_type=jnp.float32)
     value_sum = jnp.dot(tokens, v_full, preferred_element_type=jnp.float32)

time: 275 us -> 275 us (level)
  the two profiles are of different devices: /device:TPU:2 before, /device:TPU:12 now
where the time goes in v1:
time: 275 us; the launch traced here: 274 us
  waiting for transfers between devices  195 us (71%)
  local copies, waits for them, and re-layouts  27.2 us (10%)
  matrix products  22 us (8%)
  between operations  13.3 us (5%)
  starting transfers between devices  10.4 us (4%)
  other arithmetic  5.93 us (2%)
    all_gather x1, waiting for transfers between devices, per_device(): every = lax.all_gather(summary.astype(jnp.bfloat16), 'dp')  83 us
    all_gather x1, waiting for transfers between devices, per_device(): gathered = lax.all_gather(local, 'dp', axis=0, tiled=True)  57.9 us
    reduce_scatter x1, waiting for transfers between devices, per_device(): lax.psum_scatter(partial_terms.astype(jnp.bfloat16), 'mp', scatter_dimens...  44.8 us
    dot_general x1, local copies, waits for them, and re-layouts, per_device(): jnp.dot(chosen[None, :], every.reshape(blocks, -1), preferred_element_typ...  11.1 us
    reshape x1, local copies, waits for them, and re-layouts, per_device(): every.reshape(blocks, -1)  10.9 us
    all_to_all x1, starting transfers between devices, tiled_gather(): return lax.all_to_all(copies, axis, dim, dim, tiled=True)  10.3 us
    all_to_all x1, waiting for transfers between devices, tiled_gather(): return lax.all_to_all(copies, axis, dim, dim, tiled=True)  9.76 us
    dot_general x1, matrix products, per_device(): jnp.dot(chosen[None, :], every.reshape(blocks, -1), preferred_element_typ...  5.76 us
  transfers between devices with their start and end apart: 4, of which 4 were waited for; matrix products, arithmetic and copies ran while one was open for 6% of the time, Pallas kernels for 0%

profile of v1, /device:TPU:12, one launch (start us, length us, event | category | flops | bytes accessed | tf_op | source)
XLA Modules:
  0.0 274.2 jit_solution(6763296668605365871)
XLA Ops:
  6.5 0.0 copy-start
  6.5 0.0 copy-start.3
  6.5 0.0 copy-start.1
  6.5 0.0 all-gather.4.cloned.1.call-start
  6.5 1.6 pad_maximum_fusion
  8.1 0.0 all-gather.4.cloned.1.call-update
  8.2 0.8 reduce-window.4
  9.0 0.1 convert_reduce_fusion
  9.1 0.7 select_reduce_fusion
  9.8 0.0 copy-done
  9.8 2.3 constant_dynamic-update-slice_fusion.7
  12.1 0.6 constant_dynamic-update-slice_fusion.6
  12.7 0.6 constant_dynamic-update-slice_fusion.5
  13.3 0.6 constant_dynamic-update-slice_fusion.4
  14.0 0.6 constant_dynamic-update-slice_fusion.3
  14.6 0.6 constant_dynamic-update-slice_fusion.2
  15.2 0.6 constant_dynamic-update-slice_fusion.1
  15.8 0.6 constant_dynamic-update-slice_fusion
  16.4 10.3 %all-to-all-start = ((bf16[512,8,32]{0,2,1:T(8,128)(2,1)}), bf16[512,8,32]{0,2,1:T(8,128)(2,1)S(1)}, u32[]{:S(2)}, u32[]{:S(2)}) async-start(bf16[512,8,32]{0,2,1:T(8,128)(2,1)} %bitcast.4), calls=%async_computation | async-start | bytes 524288 | tf_op jit(solution)/shard_map/all_to_all | solution.py:14
  26.7 0.0 all-gather.6.cloned.1.call-start
  26.8 0.0 copy-done.3
  26.8 0.1 compare_reduce_fusion
  27.0 0.6 fusion.43
  27.6 1.2 compare_convert_fusion
  28.9 9.8 %all-to-all-done = bf16[512,8,32]{0,2,1:T(8,128)(2,1)S(1)} async-done(((bf16[512,8,32]{0,2,1:T(8,128)(2,1)}), bf16[512,8,32]{0,2,1:T(8,128)(2,1)S(1)}, u32[]{:S(2)}, u32[]{:S(2)}) %all-to-all-start) | async-done | bytes 262176 | tf_op jit(solution)/shard_map/all_to_all | solution.py:14
  38.6 0.0 copy-done.1
  38.6 0.3 fusion.44
  38.9 57.9 %all-gather.4.cloned.1.call-done = bf16[2048,576]{1,0:T(8,128)(2,1)} async-done(((bf16[32,576]{1,0:T(8,128)(2,1)}), bf16[2048,576]{1,0:T(8,128)(2,1)}) %all-gather.4.cloned.1.call-update) | async-done | bytes 2359312 | tf_op jit(solution)/shard_map/all_gather | solution.py:95
  96.8 2.1 convolution_convert_fusion.2
  98.9 0.1 multiply_convert_fusion.1
  99.0 2.5 fusion.6
  101.5 1.1 convolution_convert_fusion.1
  102.7 0.0 all-gather.6.cloned.1.call-update
  102.7 0.0 reduce-scatter.2.cloned.1.call-start
  102.8 0.6 fusion.33
  103.4 0.1 convert_reduce_fusion.1
  103.5 0.2 fusion.14
  103.7 1.8 convolution_convert_fusion.3
  105.5 0.1 multiply_convert_fusion
  105.6 1.8 fusion.2
  107.4 83.0 %all-gather.6.cloned.1.call-done = bf16[128,273,128]{2,1,0:T(8,128)(2,1)} async-done(((bf16[2,273,128]{2,1,0:T(8,128)(2,1)}), bf16[128,273,128]{2,1,0:T(8,128)(2,1)}) %all-gather.6.cloned.1.call-update) | async-done | bytes 8945680 | tf_op jit(solution)/shard_map/all_gather | solution.py:115
  190.4 10.9 %reshape.179 = bf16[64,69888]{1,0:T(8,128)(2,1)} reshape(bf16[128,273,128]{2,1,0:T(8,128)(2,1)} %all-gather.6.cloned.1.call-done) | data formatting | bytes 17891328 | tf_op jit(solution)/shard_map/reshape | solution.py:118
  201.3 11.1 %dot_general.49 = bf16[2,273,128,64]{2,1,0,3:T(8,128)(2,1)} reshape(bf16[69888,64]{0,1:T(8,128)(2,1)} %bitcast.55) | data formatting | bytes 17891328 | tf_op jit(solution)/shard_map/dot_general | solution.py:117
  212.4 0.0 copy-start.4
  212.4 5.8 %fusion = bf16[1,2,273,128]{3,0,2,1:T(2,128)(2,1)S(1)} fusion(bf16[2,273,128,64]{2,1,0,3:T(8,128)(2,1)} %dot_general.49, s32[64]{0:T(128)S(1)} %convert_reduce_fusion.1, s32[]{:T(128)} %fusion.33, s32[]{:T(128)S(6)} %axis_index.23), kind=kOutput, calls=%fused_computation | convolution fusion | flops 8945856 | bytes 9085704 | tf_op jit(solution)/shard_map/dot_general | solution.py:117
  218.2 0.0 copy-start.2
  218.2 0.0 copy-done.4
  218.2 0.5 multiply_reduce_fusion
  218.7 0.1 copy-done.2
  218.9 0.1 multiply_convert_fusion.2
  219.0 3.9 %convolution_convert_fusion = bf16[512,2048]{1,0:T(8,128)(2,1)} fusion(bf16[512,256]{0,1:T(8,128)(2,1)S(1)} %bitcast.57, bf16[2048,576]{1,0:T(8,128)(2,1)} %all-gather.4.cloned.1.call-done), kind=kOutput, calls=%fused_computation.2 | convolution fusion | flops 537919488 | bytes 3407872 | tf_op jit(solution)/shard_map/dot_general | solution.py:124
  222.9 0.0 reduce-scatter.2.cloned.1.call-update
  222.9 44.8 %reduce-scatter.2.cloned.1.call-done = bf16[512,256]{1,0:T(8,128)(2,1)} async-done(((bf16[512,2048]{1,0:T(8,128)(2,1)}), bf16[512,256]{1,0:T(8,128)(2,1)}) %reduce-scatter.2.cloned.1.call-update) | async-done | bytes 262160 | tf_op jit(solution)/shard_map/reduce_scatter | solution.py:127
  (10 shorter events, 0.1 us)
Async XLA Ops:
  6.5 3.3 %copy-start = (bf16[512,2048]{1,0:T(8,128)(2,1)S(1)}, bf16[512,2048]{1,0:T(8,128)(2,1)}, u32[]{:S(2)}) copy-start(bf16[512,2048]{1,0:T(8,128)(2,1)} %param.10) | copy-start | bytes 6291460
  6.5 20.3 %copy-start.3 = (s32[4]{0:T(128)S(1)}, s32[4]{0:T(128)}, u32[]{:S(2)}) copy-start(s32[4]{0:T(128)} %param.16) | copy-start | bytes 52
  6.5 32.1 %copy-start.1 = (bf16[256,256]{1,0:T(8,128)(2,1)S(1)}, bf16[256,256]{1,0:T(8,128)(2,1)}, u32[]{:S(2)}) copy-start(bf16[256,256]{1,0:T(8,128)(2,1)} %param.15) | copy-start | bytes 393220
  6.5 90.2 %all-gather.4.cloned.1.call-start = ((), (), s32[]{:S(2)}) async-start(), calls=%async_computation.2 | async-start | bytes 2662400 | tf_op jit(solution)/shard_map/all_gather | solution.py:95
  16.4 22.2 %all-to-all-start = ((bf16[512,8,32]{0,2,1:T(8,128)(2,1)}), bf16[512,8,32]{0,2,1:T(8,128)(2,1)S(1)}, u32[]{:S(2)}, u32[]{:S(2)}) async-start(bf16[512,8,32]{0,2,1:T(8,128)(2,1)} %bitcast.4), calls=%async_computation | async-start | bytes 524288 | tf_op jit(solution)/shard_map/all_to_all | solution.py:14
  26.7 163.7 %all-gather.6.cloned.1.call-start = ((), (), s32[]{:S(2)}) async-start(), calls=%async_computation.4 | async-start | bytes 9318400 | tf_op jit(solution)/shard_map/all_gather | solution.py:115
  102.7 165.0 %reduce-scatter.2.cloned.1.call-start = ((), (), s32[]{:S(2)}) async-start(), calls=%async_computation.3 | async-start | bytes 2359296 | tf_op jit(solution)/shard_map/reduce_scatter | solution.py:127
  212.4 5.8 %copy-start.4 = (f32[2,128,512]{2,1,0:T(8,128)S(1)}, f32[2,128,512]{2,1,0:T(8,128)}, u32[]{:S(2)}) copy-start(f32[2,128,512]{2,1,0:T(8,128)} %fusion.2) | copy-start | bytes 1572868
  218.2 0.7 copy-start.2
Sparse Core Ops, SparseCore 0:
  10.7 86.0 all-gather.3
  102.8 87.5 all-gather.5
  223.0 44.6 reduce-scatter.1
